TPU v7x, 32 devices: a whole 2x2x4 slice. The times are simulated.
32 devices in a mesh: rep: 4 (over x, core), shard: 8 (over z, y).
Axes of the slice: x: 2, y: 2, z: 4, core: 2. Of those that a mesh axis runs over, the one named last changes fastest.
Arguments:
- residual: float32 [4, 1024, 768], P('rep', 'shard'), may hold values from -6 to 6
- segment_ids: int32 [4, 1024], P('rep', 'shard'), may hold values from 0 to 7, never falling along the last dimension, each value on 1 to 256 neighbouring positions
- in_weight: bfloat16 [2, 768, 3352], P(None, 'shard'), may hold values from -0.21875 to 0.21875
- conv_weight: bfloat16 [2, 4, 1792], P(None, None, 'shard'), may hold values from -3 to 3
- conv_bias: bfloat16 [2, 1792], P(None, 'shard'), may hold values from -3 to 3
- a_log: float32 [2, 24], replicated, may hold values from -2 to 2.5
- dt_bias: float32 [2, 24], replicated, may hold values from -7 to -2
- d_skip: float32 [2, 24], replicated, may hold values from 0.5 to 1.5
- norm_gain: bfloat16 [2, 768], P(None, 'shard'), may hold values from 0.5 to 1.5
- gated_gain: bfloat16 [2, 1536], P(None, 'shard'), may hold values from 0.5 to 1.5
- out_weight: bfloat16 [2, 1536, 768], P(None, 'shard'), may hold values from -0.3125 to 0.3125
- out_cotangent: float32 [4, 1024, 768], P('rep', 'shard'), may hold values from -6 to 6
Outputs:
- output: float32 [4, 1024, 768], P('rep', 'shard')
- grad_input: float32 [4, 1024, 768], P('rep', 'shard')
- grad_in_weight: float32 [2, 768, 3352], P(None, 'shard')
- grad_conv_weight: float32 [2, 4, 1792], P(None, None, 'shard')
- grad_conv_bias: float32 [2, 1792], P(None, 'shard')
- grad_a_log: float32 [2, 24], replicated
- grad_dt_bias: float32 [2, 24], replicated
- grad_d_skip: float32 [2, 24], replicated
- grad_norm_gain: float32 [2, 768], P(None, 'shard')
- grad_gated_gain: float32 [2, 1536], P(None, 'shard')
- grad_out_weight: float32 [2, 1536, 768], P(None, 'shard')
Inputs may be any that keep to these rules, and one draw needn't show every extreme that they name: `segment_ids`: in each sequence the ids never fall; each document has 1 to 256 tokens and one has exactly 256.
All inputs are finite; a program needn't handle non-finite values.
Results may differ from a plain program's by a relative error of at most 0.011.
Values may be sent and summed in bfloat16 or wider, within the bound.
No kernel may reach another device: no remote copies, remote signals or barrier semaphores. Data moves between devices by JAX's collectives and lax.ppermute only.
A program may use at most 256 MiB of HBM per device.

v0:
```python
from functools import partial
import jax
import jax.numpy as jnp
from jax import lax
from jax.sharding import PartitionSpec as P

HEADS = 24
STATE = 128
HEADDIM = 64
CONV = 4
SPAN = 128
INNER = 1536
CONVDIM = 1792
EPS = 1e-05
HIGH = lax.Precision.HIGHEST


def passed_along(x, axis, by):
    count = lax.axis_size(axis)
    pairs = [(i, i + by) for i in range(count) if 0 <= i + by < count]
    return lax.ppermute(x, axis, pairs)


def carried_in(part, axis, combine, identity, reverse):
    count = lax.axis_size(axis)
    place = lax.axis_index(axis)
    ahead = count - 1 - place if reverse else place
    gathered = jax.tree.map(lambda a: lax.all_gather(a, axis), part)
    state = jax.tree.map(lambda a, e: jnp.zeros_like(a) + jnp.asarray(e, a.dtype), part, identity)

    def one(turn, state):
        source = count - 1 - turn if reverse else turn
        return combine(
            state, jax.tree.map(lambda a: lax.dynamic_index_in_dim(a, source, 0, False), gathered)
        )

    return lax.fori_loop(0, ahead, one, state)


def rms(values, gain):
    return values * lax.rsqrt(jnp.mean(values * values, axis=-1, keepdims=True) + EPS) * gain


def span_step(carry, pieces):
    state, last = carry
    xs, bs, cs, dts, das, segs = pieces
    width = segs.shape[0]
    cum = jnp.cumsum(das, axis=0)
    rows = lax.broadcasted_iota(jnp.int32, (width, width), 0)
    cols = lax.broadcasted_iota(jnp.int32, (width, width), 1)
    mask = ((rows >= cols) & (segs[:, None] == segs[None, :])).astype(jnp.float32)
    cum_t = cum.T
    diff = cum_t[:, :, None] - cum_t[:, None, :]
    lmat = jnp.exp(jnp.where(mask[None] > 0, diff, 0.0)) * mask[None]
    scores = jnp.dot(cs, bs.T, precision=HIGH)
    mixing = lmat * scores[None] * dts.T[:, None, :]
    inside = jnp.einsum("hij,jhp->ihp", mixing, xs, precision=HIGH)
    valid = (segs == last).astype(jnp.float32)
    carried = jnp.einsum("in,hnp->ihp", cs, state, precision=HIGH)
    carried = carried * (jnp.exp(cum) * valid[:, None])[:, :, None]
    tail = (segs == segs[-1]).astype(jnp.float32)
    decay = jnp.exp(cum[-1][None, :] - cum) * tail[:, None] * dts
    keep = jnp.exp(cum[-1]) * (segs[-1] == last).astype(jnp.float32)
    fresh = jnp.einsum("jh,jn,jhp->hnp", decay, bs, xs, precision=HIGH)
    return ((state * keep[:, None, None] + fresh, segs[-1]), inside + carried)


def front(xbc, rim, dt_raw, conv_w, conv_b, dtb, alog, keeps):
    length = xbc.shape[0]
    padded = jnp.concatenate([rim, xbc], 0)
    total = conv_b
    for k in range(CONV):
        total = total + conv_w[k] * padded[k : k + length] * keeps[k][:, None]
    conv_out = jax.nn.silu(total)
    xs = conv_out[:, :INNER].reshape(length, HEADS, HEADDIM)
    bs = conv_out[:, INNER : INNER + STATE]
    cs = conv_out[:, INNER + STATE :]
    dts = jax.nn.softplus(dt_raw + dtb)
    return (xs, bs, cs, dts, -dts * jnp.exp(alog))


def local_states(xs, bs, cs, dts, das, seg, seg_prev):
    length = seg.shape[0]
    count = length // SPAN
    pieces = (
        xs.reshape(count, SPAN, HEADS, HEADDIM),
        bs.reshape(count, SPAN, STATE),
        cs.reshape(count, SPAN, STATE),
        dts.reshape(count, SPAN, HEADS),
        das.reshape(count, SPAN, HEADS),
        seg.reshape(count, SPAN),
    )
    start = (jnp.zeros((HEADS, STATE, HEADDIM), jnp.float32), seg[0])
    (final, _), ys = lax.scan(span_step, start, pieces)
    passing = jnp.exp(jnp.sum(das, axis=0)) * (seg[-1] == seg_prev).astype(jnp.float32)
    return (ys.reshape(length, HEADS, HEADDIM), passing, final)


def finish(z_part, xs, cs, das, y_local, entering, dskip, ggain, seg, seg_prev):
    length = seg.shape[0]
    cum = jnp.cumsum(das, axis=0)
    valid = (seg == seg_prev).astype(jnp.float32)
    from_before = jnp.einsum("tn,hnp->thp", cs, entering, precision=HIGH)
    from_before = from_before * (jnp.exp(cum) * valid[:, None])[:, :, None]
    ys = y_local + from_before + dskip[None, :, None] * xs
    gated = ys.reshape(length, INNER) * jax.nn.silu(z_part)
    return rms(gated, ggain)


def combine(earlier, later):
    return (earlier[0] * later[0], later[0][:, None, None] * earlier[1] + later[1])


def gather_layer(
    in_weight, out_weight, conv_weight, conv_bias, norm_gain, gated_gain, layer, again
):
    if again:
        return (
            lax.all_gather(in_weight[layer], "shard", axis=0, tiled=True),
            lax.all_gather(out_weight[layer], "shard", axis=0, tiled=True),
            lax.all_gather(conv_weight[layer], "shard", axis=1, tiled=True),
            lax.all_gather(conv_bias[layer], "shard", axis=0, tiled=True),
            lax.all_gather(norm_gain[layer], "shard", axis=0, tiled=True),
            lax.all_gather(gated_gain[layer], "shard", axis=0, tiled=True),
        )
    return (
        lax.all_gather(in_weight[layer], "shard", axis=0, tiled=True),
        lax.all_gather(out_weight[layer], "shard", axis=0, tiled=True),
        lax.all_gather(conv_weight[layer], "shard", axis=1, tiled=True),
        lax.all_gather(conv_bias[layer], "shard", axis=0, tiled=True),
        lax.all_gather(norm_gain[layer], "shard", axis=0, tiled=True),
        lax.all_gather(gated_gain[layer], "shard", axis=0, tiled=True),
    )


def per_device(
    residual,
    segment_ids,
    in_weight,
    conv_weight,
    conv_bias,
    a_log,
    dt_bias,
    d_skip,
    norm_gain,
    gated_gain,
    out_weight,
    out_cotangent,
):
    u_now = residual[0]
    seg = segment_ids[0]
    length = seg.shape[0]
    layers = in_weight.shape[0]
    rim_ids = passed_along(seg[length - CONV + 1 :], "shard", 1)
    seg_ext = jnp.concatenate([rim_ids, seg])
    seg_prev = rim_ids[CONV - 2]
    keeps = jnp.stack([(seg_ext[k : k + length] == seg).astype(jnp.float32) for k in range(CONV)])
    identity = (jnp.ones((HEADS,), jnp.float32), jnp.zeros((HEADS, STATE, HEADDIM), jnp.float32))
    saved = []
    for layer in range(layers):
        weights = gather_layer(
            in_weight, out_weight, conv_weight, conv_bias, norm_gain, gated_gain, layer, False
        )
        w_in, w_out, conv_w, conv_b, n_gain, g_gain = weights
        normed, norm_pull = jax.vjp(rms, u_now, n_gain.astype(jnp.float32))
        hidden = normed.astype(jnp.bfloat16)
        proj = jnp.dot(hidden, w_in, preferred_element_type=jnp.float32)
        z_part = proj[:, :INNER]
        xbc = proj[:, INNER : INNER + CONVDIM]
        dt_raw = proj[:, INNER + CONVDIM :]
        rim = passed_along(xbc[length - CONV + 1 :], "shard", 1)
        feats, front_pull = jax.vjp(
            partial(front, keeps=keeps),
            xbc,
            rim,
            dt_raw,
            conv_w.astype(jnp.float32),
            conv_b.astype(jnp.float32),
            dt_bias[layer],
            a_log[layer],
        )
        xs, bs, cs, dts, das = feats
        (y_local, passing, final), local_pull = jax.vjp(
            partial(local_states, seg=seg, seg_prev=seg_prev), xs, bs, cs, dts, das
        )
        entering = carried_in((passing, final), "shard", combine, identity, False)[1]
        yn, finish_pull = jax.vjp(
            partial(finish, seg=seg, seg_prev=seg_prev),
            z_part,
            xs,
            cs,
            das,
            y_local,
            entering,
            d_skip[layer],
            g_gain.astype(jnp.float32),
        )
        yn_b = yn.astype(jnp.bfloat16)
        u_now = u_now + jnp.dot(yn_b, w_out, preferred_element_type=jnp.float32)
        kept = None
        saved.append(
            (hidden, norm_pull, front_pull, local_pull, finish_pull, passing, entering, yn_b, kept)
        )
    grad = out_cotangent[0]
    owned = [None] * layers
    heads = [None] * layers
    for layer in reversed(range(layers)):
        hidden, norm_pull, front_pull, local_pull, finish_pull, passing, entering, yn_b, kept = (
            saved[layer]
        )
        weights = gather_layer(
            in_weight, out_weight, conv_weight, conv_bias, norm_gain, gated_gain, layer, True
        )
        w_in, w_out = (weights[0], weights[1])
        grad_b = grad.astype(jnp.bfloat16)
        g_out = jnp.dot(yn_b.T, grad_b, preferred_element_type=jnp.float32)
        d_yn = jnp.dot(grad_b, w_out.T, preferred_element_type=jnp.float32)
        d_z, d_xs1, d_cs1, d_das1, d_local, d_enter, g_dsk, g_gg = finish_pull(d_yn)
        later = carried_in((passing, d_enter), "shard", combine, identity, True)[1]
        d_passing = jnp.sum(later * entering, axis=(1, 2))
        d_xs2, d_bs, d_cs2, d_dts, d_das2 = local_pull((d_local, d_passing, later))
        d_xbc, d_rim, d_dtr, g_cw, g_cb, g_dtb, g_alog = front_pull(
            (d_xs1 + d_xs2, d_bs, d_cs1 + d_cs2, d_dts, d_das1 + d_das2)
        )
        back_rim = passed_along(d_rim, "shard", -1)
        d_xbc = d_xbc.at[length - CONV + 1 :].add(back_rim)
        d_proj = jnp.concatenate([d_z, d_xbc, d_dtr], 1).astype(jnp.bfloat16)
        g_in = jnp.dot(hidden.T, d_proj, preferred_element_type=jnp.float32)
        d_h = jnp.dot(d_proj, w_in.T, preferred_element_type=jnp.float32)
        d_u, g_ng = norm_pull(d_h)
        grad = grad + d_u
        shares = (
            lax.psum_scatter(g_in, "shard", scatter_dimension=0, tiled=True),
            lax.psum_scatter(g_out, "shard", scatter_dimension=0, tiled=True),
            lax.psum_scatter(g_cw, "shard", scatter_dimension=1, tiled=True),
            lax.psum_scatter(g_cb, "shard", scatter_dimension=0, tiled=True),
            lax.psum_scatter(g_ng, "shard", scatter_dimension=0, tiled=True),
            lax.psum_scatter(g_gg, "shard", scatter_dimension=0, tiled=True),
        )
        shares = lax.psum((shares[0], shares[1], shares[2], shares[3], shares[4], shares[5]), "rep")
        owned[layer] = shares
        heads[layer] = jnp.stack([g_alog, g_dtb, g_dsk])
    grads_in = jnp.stack([owned[k][0] for k in range(layers)])
    grads_out = jnp.stack([owned[k][1] for k in range(layers)])
    grads_cw = jnp.stack([owned[k][2] for k in range(layers)])
    grads_cb = jnp.stack([owned[k][3] for k in range(layers)])
    grads_ng = jnp.stack([owned[k][4] for k in range(layers)])
    grads_gg = jnp.stack([owned[k][5] for k in range(layers)])
    head_sums = lax.psum(jnp.stack(heads), ("rep", "shard"))
    return (
        u_now[None],
        grad[None],
        grads_in,
        grads_cw,
        grads_cb,
        head_sums[:, 0],
        head_sums[:, 1],
        head_sums[:, 2],
        grads_ng,
        grads_gg,
        grads_out,
    )


def solution(mesh):
    return jax.shard_map(
        per_device,
        mesh=mesh,
        in_specs=(
            P("rep", "shard", None),
            P("rep", "shard"),
            P(None, "shard", None),
            P(None, None, "shard"),
            P(None, "shard"),
            P(),
            P(),
            P(),
            P(None, "shard"),
            P(None, "shard"),
            P(None, "shard", None),
            P("rep", "shard", None),
        ),
        out_specs=(
            P("rep", "shard", None),
            P("rep", "shard", None),
            P(None, "shard", None),
            P(None, None, "shard"),
            P(None, "shard"),
            P(),
            P(),
            P(),
            P(None, "shard"),
            P(None, "shard"),
            P(None, "shard", None),
        ),
        check_vma=False,
    )
```

profile of v0, /device:TPU:0, one launch (start us, length us, event | category | flops | bytes accessed | tf_op | source)
XLA Modules:
  0.0 1677.2 jit_solution(14095411536137109909)
XLA Ops:
  9.9 4.9 collective-permute-start.1
  18.8 37.3 %all-reduce.43 = (bf16[768]{0:T(1024)(128)(2,1)S(1)}, bf16[1792]{0:T(1024)(128)(2,1)S(1)}, bf16[1536]{0:T(1024)(128)(2,1)S(1)}, bf16[768]{0:T(1024)(128)(2,1)S(1...) all-reduce(bf16[768]{0:T(1024)(128)(2,1)S(1)} %dynamic-update-slice, ...), channel_id=4, replica_groups=mesh['rep'=4,'shard'=8] {'shard'}, use_global_device_ids=true, to_apply=%add.27 | all-reduce | flops 8192 | bytes 32768
  56.3 36.0 %all-gather.1 = bf16[1,4,1792]{1,0,2:T(2,128)(2,1)S(1)} all-gather(bf16[1,4,224]{1,0,2:T(2,128)(2,1)S(1)} %copy.431), channel_id=3, replica_groups=mesh['rep'=4,'shard'=8] {'shard'}, dimensions={2}, use_global_device_ids=true | all-gather | bytes 16128 | tf_op jit(solution)/shard_map/all_gather | solution.py:129
  96.0 37.5 %slice_reduce_fusion.7 = (f32[1792]{0:T(1024)S(1)}, f32[1792]{0:T(1024)S(1)}, f32[1792]{0:T(1024)S(1)}, f32[1792]{0:T(1024)S(1)}) fusion(f32[1,4,1792]{1,0,2:T(1,128)S(1)} %convert_element_type.131), kind=kLoop, calls=%fused_computation.128 | loop fusion | bytes 57344 | tf_op jit(solution)/shard_map/jvp()/slice | solution.py:73
  146.3 5.4 fusion.102
  158.1 36.8 %all-gather.9 = bf16[1,4,1792]{1,0,2:T(2,128)(2,1)S(1)} all-gather(bf16[1,4,224]{1,0,2:T(2,128)(2,1)S(1)} %copy.432), channel_id=11, replica_groups=mesh['rep'=4,'shard'=8] {'shard'}, dimensions={2}, use_global_device_ids=true | all-gather | bytes 16128 | tf_op jit(solution)/shard_map/all_gather | solution.py:129
  197.8 37.7 %slice_reduce_fusion.3 = (f32[1792]{0:T(1024)}, f32[1792]{0:T(1024)}, f32[1792]{0:T(1024)}, f32[1792]{0:T(1024)}) fusion(f32[1,4,1792]{1,0,2:T(1,128)S(1)} %convert_element_type.135), kind=kLoop, calls=%fused_computation.123 | loop fusion | bytes 57344 | tf_op jit(solution)/shard_map/jvp()/slice | solution.py:73
  236.9 19.7 %all-reduce.28 = f32[192]{0:T(256)S(1)} all-reduce(f32[192]{0:T(256)S(1)} %multiply_dynamic-update-slice_fusion.1), channel_id=6, replica_groups=mesh['rep'=4,'shard'=8] {'shard'}, use_global_device_ids=true, to_apply=%add.28 | all-reduce | flops 192 | bytes 1536
  269.5 43.2 %all-gather.31.cloned.1.call-done = bf16[1,1536,768]{2,1,0:T(8,128)(2,1)} async-done(((bf16[1,192,768]{2,1,0:T(8,128)(2,1)}), bf16[1,1536,768]{2,1,0:T(8,128)(2,1)}) %all-gather.31.cloned.1.call-update) | async-done | bytes 2359312 | tf_op jit(solution)/shard_map/all_gather | solution.py:128
  315.9 84.1 %all-gather.33.cloned.1.call-done = bf16[1,768,3352]{2,1,0:T(8,128)(2,1)} async-done(((bf16[1,96,3352]{2,1,0:T(8,128)(2,1)}), bf16[1,768,3352]{2,1,0:T(8,128)(2,1)}) %all-gather.33.cloned.1.call-update) | async-done | bytes 5148688 | tf_op jit(solution)/shard_map/all_gather | solution.py:127
  417.6 5.4 fusion.101
  426.5 19.1 %all-reduce.32 = f32[192]{0:T(256)S(1)} all-reduce(f32[192]{0:T(256)S(1)} %multiply_dynamic-update-slice_fusion), channel_id=14, replica_groups=mesh['rep'=4,'shard'=8] {'shard'}, use_global_device_ids=true, to_apply=%add.32 | all-reduce | flops 192 | bytes 1536
  447.8 75.4 %all-gather.35.cloned.1.call-done = f32[192,128,64]{1,2,0:T(8,128)} async-done(((f32[24,128,64]{1,2,0:T(8,128)}), f32[192,128,64]{1,2,0:T(8,128)}) %all-gather.35.cloned.1.call-update) | async-done | bytes 6291472 | tf_op jit(solution)/shard_map/all_gather | solution.py:28
  535.1 40.7 %all-gather.37.cloned.1.call-done = bf16[1,1536,768]{2,1,0:T(8,128)(2,1)} async-done(((bf16[1,192,768]{2,1,0:T(8,128)(2,1)}), bf16[1,1536,768]{2,1,0:T(8,128)(2,1)}) %all-gather.37.cloned.1.call-update) | async-done | bytes 2359312 | tf_op jit(solution)/shard_map/all_gather | solution.py:128
  594.6 91.4 %all-gather.39.cloned.1.call-done = f32[192,128,64]{1,2,0:T(8,128)} async-done(((f32[24,128,64]{1,2,0:T(8,128)}), f32[192,128,64]{1,2,0:T(8,128)}) %all-gather.39.cloned.1.call-update) | async-done | bytes 6291472 | tf_op jit(solution)/shard_map/all_gather | solution.py:28
  687.4 50.6 %while.36 = (s32[]{:T(128)}, f32[24,128,64]{2,1,0:T(8,128)}, s32[]{:T(128)}, f32[8,24]{1,0:T(8,128)}, f32[8,24,128,64]{2,3,1,0:T(8,128)}, /*index=5*/s32[]{:T(128)}, s32[]{:T(128)}, s32[]{:T(128)}, s32[]{:T(128)}) while((s32[]{:T(128)}, f32[24,128,64]{2,1,0:T(8,128)}, s32[]{:T(128)}, f32[8,24]{1,0:T(8,128)}, f32[8,24,128,64]{2,3,1,0:T(8,128)}, ...), condition=%wide.region_15.17_spmd, body=%wide.region_14.16_spmd.sunk | while | flops 393222 | bytes 5505467 | solution.py:37
  773.8 6.0 scatter-add.6
  779.9 5.1 multiply_reduce_fusion.30
  808.5 6.7 fusion.173
  830.1 59.3 %all-gather.41.cloned.1.call-done = f32[192,128,64]{1,2,0:T(8,128)} async-done(((f32[24,128,64]{1,2,0:T(8,128)}), f32[192,128,64]{1,2,0:T(8,128)}) %all-gather.41.cloned.1.call-update) | async-done | bytes 6291472 | tf_op jit(solution)/shard_map/all_gather | solution.py:28
  890.7 50.3 %while.37 = (s32[]{:T(128)}, f32[24,128,64]{2,1,0:T(8,128)}, s32[]{:T(128)}, f32[8,24]{1,0:T(8,128)}, f32[8,24,128,64]{2,3,1,0:T(8,128)}, /*index=5*/s32[]{:T(128)}, s32[]{:T(128)}, s32[]{:T(128)}, s32[]{:T(128)}) while((s32[]{:T(128)}, f32[24,128,64]{2,1,0:T(8,128)}, s32[]{:T(128)}, f32[8,24]{1,0:T(8,128)}, f32[8,24,128,64]{2,3,1,0:T(8,128)}, ...), condition=%wide.region_30.32_spmd, body=%wide.region_29.31_spmd.sunk | while | flops 393222 | bytes 5505467 | solution.py:37
  941.0 5.3 multiply_reduce_fusion.16
  989.4 6.0 scatter-add.9
  995.4 6.7 fusion.172
  1010.4 42.3 %reduce-scatter.17.cloned.1.call-done = f32[192,768]{1,0:T(8,128)} async-done(((f32[1536,768]{1,0:T(8,128)}), f32[192,768]{1,0:T(8,128)}) %reduce-scatter.17.cloned.1.call-update) | async-done | bytes 589840 | tf_op jit(solution)/shard_map/reduce_scatter | solution.py:234
  1052.7 99.0 %reduce-scatter.15.cloned.1.call-done = f32[192,768]{1,0:T(8,128)} async-done(((f32[1536,768]{1,0:T(8,128)}), f32[192,768]{1,0:T(8,128)}) %reduce-scatter.15.cloned.1.call-update) | async-done | bytes 589840 | tf_op jit(solution)/shard_map/reduce_scatter | solution.py:234
  1151.7 183.2 %reduce-scatter.13.cloned.1.call-done = f32[96,3352]{1,0:T(8,128)} async-done(((f32[768,3352]{1,0:T(8,128)}), f32[96,3352]{1,0:T(8,128)}) %reduce-scatter.13.cloned.1.call-update) | async-done | bytes 1287184 | tf_op jit(solution)/shard_map/reduce_scatter | solution.py:233
  1334.9 182.8 %reduce-scatter.11.cloned.1.call-done = f32[96,3352]{1,0:T(8,128)} async-done(((f32[768,3352]{1,0:T(8,128)}), f32[96,3352]{1,0:T(8,128)}) %reduce-scatter.11.cloned.1.call-update) | async-done | bytes 1287184 | tf_op jit(solution)/shard_map/reduce_scatter | solution.py:233
  1517.8 39.6 %psum.97 = f32[2,3,24]{2,1,0:T(4,128)S(1)} all-reduce(f32[2,3,24]{2,1,0:T(4,128)S(1)} %pad_maximum_fusion.11), channel_id=1, replica_groups=mesh['rep'=4,'shard'=8] {'rep','shard'}, use_global_device_ids=true, to_apply=%region_72.74 | all-reduce | flops 144 | bytes 1152 | tf_op jit(solution)/shard_map/psum | solution.py:249
  1562.4 37.4 %all-reduce.40 = (f32[1792]{0:T(1024)S(1)}, f32[1792]{0:T(1024)S(1)}, f32[768]{0:T(1024)S(1)}, f32[768]{0:T(1024)S(1)}, f32[1536]{0:T(1024)S(1)}, /*index=5*/f32[1536]{0:T(1024)S(1)}) all-reduce(f32[1792]{0:T(1024)S(1)} %copy-done.120, f32[1792]{0:T(1024)S(1)} %get-tuple-element.833, ...), channel_id=25, replica_groups=mesh['rep'=4,'shard'=8] {'shard'}, use_global_device_ids=true, to_apply=%region_62.64.clone | all-reduce | flops 8192 | bytes 65536
  1602.1 11.7 all-reduce.41
  1616.1 49.8 %all-reduce.46.cloned.1.call-done = (f32[1,96,3352]{2,1,0:T(8,128)}, f32[1,96,3352]{2,1,0:T(8,128)}, f32[1,192,768]{2,1,0:T(8,128)}, f32[1,192,768]{2,1,0:T(8,128)}) async-done(((f32[1,96,3352]{2,1,0:T(8,128)}, f32[1,96,3352]{2,1,0:T(8,128)}, f32[1,192,768]{2,1,0:T(8,128)}, f32[1,192,768]{2,1,0:T(8,128)}), (f32[1,96,3352]{2,1,0:T(8,128)}, f32[1,96,3352]{2,1,0:T(8,128)}, f32[1,192,768]{2,1,0:T(8,128)}, ...) | async-done | bytes 3754000 | tf_op jit(solution)/shard_map/psum | solution.py:240
  (745 shorter events, 337.1 us)
Async XLA Ops:
  7.2 48.9 %copy-start.193 = (bf16[2,4,224]{2,1,0:T(4,128)(2,1)S(1)}, bf16[2,4,224]{2,1,0:T(4,128)(2,1)}, u32[]{:S(2)}) copy-start(bf16[2,4,224]{2,1,0:T(4,128)(2,1)} %param.28) | copy-start | bytes 10756
  7.2 129.0 %all-gather.27.cloned.1.call-start = ((), (), s32[]{:S(2)}) async-start(), calls=%async_computation.10 | async-start | bytes 5971968 | tf_op jit(solution)/shard_map/all_gather | solution.py:127
  9.8 250.9 %all-gather.29.cloned.1.call-start = ((), (), s32[]{:S(2)}) async-start(), calls=%async_computation.11 | async-start | bytes 7077888 | tf_op jit(solution)/shard_map/all_gather | solution.py:28
  9.9 123.7 %collective-permute-start.1 = (s32[3]{0:T(128)S(1)}, s32[3]{0:T(128)S(1)}, u32[]{:S(2)}, u32[]{:S(2)}) collective-permute-start(s32[3]{0:T(128)S(1)} %slice_bitcast_fusion.5), channel_id=1, source_target_pairs={{0,1},{1,2},{2,3},{3,4},{4,5},{5,6},{6,7},{8,9},{9,10},{10,11},{11... | collective-permute-start | bytes 44 | tf_op jit(solution)/shard_map/ppermute | solution.py:21
  14.8 80.4 %copy-start.30 = (f32[1,128,768]{2,1,0:T(8,128)S(1)}, f32[1,128,768]{2,1,0:T(8,128)}, u32[]{:S(2)}) copy-start(f32[1,128,768]{2,1,0:T(8,128)} %param.25) | copy-start | bytes 1179652
  96.0 46.9 %copy-start.182 = (f32[24]{0:T(128)}, f32[24]{0:T(128)S(1)}, u32[]{:S(2)}) copy-start(f32[24]{0:T(128)S(1)} %get-tuple-element.1008) | copy-start | bytes 292
  96.0 48.3 %copy-start.138 = (f32[24]{0:T(128)}, f32[24]{0:T(128)S(1)}, u32[]{:S(2)}) copy-start(f32[24]{0:T(128)S(1)} %get-tuple-element.984) | copy-start | bytes 292
  141.6 3.4 collective-permute-start
  143.7 93.1 %copy-start.185 = (f32[24]{0:T(128)}, f32[24]{0:T(128)S(1)}, u32[]{:S(2)}) copy-start(f32[24]{0:T(128)S(1)} %get-tuple-element.939) | copy-start | bytes 292
  151.7 107.2 %copy-start.25 = (f32[128,1792]{0,1:T(8,128)}, f32[128,1792]{0,1:T(8,128)S(1)}, u32[]{:S(2)}) copy-start(f32[128,1792]{0,1:T(8,128)S(1)} %get-tuple-element.941) | copy-start | bytes 2752516
  154.5 158.2 %all-gather.31.cloned.1.call-start = ((), (), s32[]{:S(2)}) async-start(), calls=%async_computation.12 | async-start | bytes 2654208 | tf_op jit(solution)/shard_map/all_gather | solution.py:128
  155.4 244.6 %all-gather.33.cloned.1.call-start = ((), (), s32[]{:S(2)}) async-start(), calls=%async_computation.13 | async-start | bytes 5971968 | tf_op jit(solution)/shard_map/all_gather | solution.py:127
  156.0 367.2 %all-gather.35.cloned.1.call-start = ((), (), s32[]{:S(2)}) async-start(), calls=%async_computation.14 | async-start | bytes 7077888 | tf_op jit(solution)/shard_map/all_gather | solution.py:28
  315.9 84.1 %copy-start.211 = (f32[128]{0:T(128)}, f32[128]{0:T(128)S(1)}, u32[]{:S(2)}) copy-start(f32[128]{0:T(128)S(1)} %get-tuple-element.998) | copy-start | bytes 1540
  315.9 88.9 %copy-start.179 = (f32[128]{0:T(128)}, f32[128]{0:T(128)S(1)}, u32[]{:S(2)}) copy-start(f32[128]{0:T(128)S(1)} %fusion.221) | copy-start | bytes 1540
  408.4 7.1 collective-permute-start.2
  425.7 150.1 %all-gather.37.cloned.1.call-start = ((), (), s32[]{:S(2)}) async-start(), calls=%async_computation.15 | async-start | bytes 2654208 | tf_op jit(solution)/shard_map/all_gather | solution.py:128
  426.3 259.7 %all-gather.39.cloned.1.call-start = ((), (), s32[]{:S(2)}) async-start(), calls=%async_computation.16 | async-start | bytes 7077888 | tf_op jit(solution)/shard_map/all_gather | solution.py:28
  426.4 152.8 %copy-start.73 = (f32[1536]{0:T(1024)}, f32[1536]{0:T(1024)S(1)}, u32[]{:S(2)}) copy-start(f32[1536]{0:T(1024)S(1)} %convert_element_type.143) | copy-start | bytes 18436
  445.7 143.3 %copy-start.164 = (f32[24,128]{1,0:T(8,128)}, f32[24,128]{1,0:T(8,128)S(1)}, u32[]{:S(2)}) copy-start(f32[24,128]{1,0:T(8,128)S(1)} %copy.318) | copy-start | bytes 36868
  446.1 143.0 %copy-start.102 = (f32[128,128]{1,0:T(8,128)}, f32[128,128]{1,0:T(8,128)S(1)}, u32[]{:S(2)}) copy-start(f32[128,128]{1,0:T(8,128)S(1)} %fusion.189) | copy-start | bytes 196612
  584.1 305.3 %all-gather.41.cloned.1.call-start = ((), (), s32[]{:S(2)}) async-start(), calls=%async_computation.17 | async-start | bytes 7077888 | tf_op jit(solution)/shard_map/all_gather | solution.py:28
  765.6 5.8 collective-permute-start.3
  792.6 215.3 %reduce-scatter.21.cloned.1.call-start = ((), (), s32[]{:S(2)}) async-start(), calls=%async_computation.19 | async-start | bytes 1032192
  798.2 254.5 %reduce-scatter.17.cloned.1.call-start = ((), (), s32[]{:S(2)}) async-start(), calls=%async_computation.9 | async-start | bytes 5308416 | tf_op jit(solution)/shard_map/reduce_scatter | solution.py:234
  802.4 349.2 %reduce-scatter.15.cloned.1.call-start = ((), (), s32[]{:S(2)}) async-start(), calls=%async_computation.8 | async-start | bytes 5308416 | tf_op jit(solution)/shard_map/reduce_scatter | solution.py:234
  807.6 527.4 %reduce-scatter.13.cloned.1.call-start = ((), (), s32[]{:S(2)}) async-start(), calls=%async_computation.7 | async-start | bytes 11943936 | tf_op jit(solution)/shard_map/reduce_scatter | solution.py:233
  815.3 702.4 %reduce-scatter.11.cloned.1.call-start = ((), (), s32[]{:S(2)}) async-start(), calls=%async_computation.6 | async-start | bytes 11943936 | tf_op jit(solution)/shard_map/reduce_scatter | solution.py:233
  828.3 62.4 %copy-start.71 = (f32[128,128]{1,0:T(8,128)}, f32[128,128]{1,0:T(8,128)S(1)}, u32[]{:S(2)}) copy-start(f32[128,128]{1,0:T(8,128)S(1)} %get-tuple-element.823) | copy-start | bytes 196612
  979.8 6.2 collective-permute-start.4
  1002.2 599.0 %reduce-scatter.19.cloned.1.call-start = ((), (), s32[]{:S(2)}) async-start(), calls=%async_computation.18 | async-start | bytes 1032192
  1010.3 655.6 %all-reduce.46.cloned.1.call-start = ((), (), s32[]{:S(2)}) async-start(), calls=%async_computation.20 | async-start | bytes 7667712 | tf_op jit(solution)/shard_map/psum | solution.py:240
  (202 other events, 1522.9 us)
Sparse Core Ops, SparseCore 0:
  10.8 104.5 all-gather.26
  154.6 105.1 all-gather.28
  262.6 50.0 all-gather.30
  314.7 85.2 all-gather.32
  425.8 97.3 all-gather.34
  525.8 49.9 all-gather.36
  584.2 101.7 all-gather.38
  792.7 96.5 all-gather.40
  892.7 62.0 reduce-scatter.20
  958.2 94.4 reduce-scatter.16
  1056.3 95.2 reduce-scatter.14
  1155.1 179.7 reduce-scatter.12
  1338.5 179.1 reduce-scatter.10
  1521.5 62.8 reduce-scatter.18
  1586.9 78.9 all-reduce.45
where the time goes:
time: 1680 us
  waiting for transfers between devices  956 us (57%)
  blocking collectives  238 us (14%)
  local copies, waits for them, and re-layouts  216 us (13%)
  other arithmetic  118 us (7%)
  matrix products  112 us (7%)
  between operations  24.3 us (1%)
    reduce_scatter x2, waiting for transfers between devices, per_device(): lax.psum_scatter(g_in, 'shard', scatter_dimension=0, tiled=True)  366 us
    all_gather x4, waiting for transfers between devices, carried_in(): gathered = jax.tree.map(lambda a: lax.all_gather(a, axis), part)  226 us
    reduce_scatter x2, waiting for transfers between devices, per_device(): lax.psum_scatter(g_out, 'shard', scatter_dimension=0, tiled=True)  141 us
    unnamed x4, blocking collectives  114 us
    all_gather x2, waiting for transfers between devices, gather_layer(): lax.all_gather(in_weight[layer], 'shard', axis=0, tiled=True)  84.1 us
    all_gather x2, waiting for transfers between devices, gather_layer(): lax.all_gather(out_weight[layer], 'shard', axis=0, tiled=True)  83.9 us
    slice x2, local copies, waits for them, and re-layouts, front(): total = total + conv_w[k] * padded[k:k + length] * keeps[k][:, None]  75.2 us
    all_gather x2, blocking collectives, gather_layer(): lax.all_gather(conv_weight[layer], 'shard', axis=1, tiled=True)  72.8 us
  transfers between devices with their start and end apart: 20, of which 13 were waited for; matrix products, arithmetic and copies ran while one was open for 17% of the time, Pallas kernels for 0%

commit v1 on v0

--- a/solution.py
+++ b/solution.py
@@ -13,6 +13,22 @@
 CONVDIM = 1792
 EPS = 1e-05
 HIGH = lax.Precision.HIGHEST
+
+
+def ring_gather(x, axis, dim):
+    ways, here, step = (lax.axis_size(axis), lax.axis_index(axis), x.shape[dim])
+    dims = [n * ways if d == dim else n for d, n in enumerate(x.shape)]
+    full = lax.dynamic_update_slice_in_dim(jnp.zeros(dims, x.dtype), x, here * step, axis=dim)
+    going_up = going_down = x
+    for far in range(1, ways // 2 + 1):
+        going_up = lax.ppermute(going_up, axis, [(d, (d + 1) % ways) for d in range(ways)])
+        full = lax.dynamic_update_slice_in_dim(full, going_up, (here - far) % ways * step, axis=dim)
+        if 2 * far < ways:
+            going_down = lax.ppermute(going_down, axis, [(d, (d - 1) % ways) for d in range(ways)])
+            full = lax.dynamic_update_slice_in_dim(
+                full, going_down, (here + far) % ways * step, axis=dim
+            )
+    return full
 
 
 def passed_along(x, axis, by):
@@ -124,7 +140,7 @@
             lax.all_gather(gated_gain[layer], "shard", axis=0, tiled=True),
         )
     return (
-        lax.all_gather(in_weight[layer], "shard", axis=0, tiled=True),
+        ring_gather(in_weight[layer], "shard", 0),
         lax.all_gather(out_weight[layer], "shard", axis=0, tiled=True),
         lax.all_gather(conv_weight[layer], "shard", axis=1, tiled=True),
         lax.all_gather(conv_bias[layer], "shard", axis=0, tiled=True),

time: 1680 us -> 1860 us (1.11)
  blocking collectives: 238 us -> 294 us
  waiting for transfers between devices: 956 us -> 1010 us
  starting transfers between devices: 12.8 us -> 63.2 us
  local copies, waits for them, and re-layouts: 216 us -> 235 us
    ppermute x0 -> x14, waiting for transfers between devices: none -> 83.2 us  [the longest x8 83.2 us: ring_gather(): lax.ppermute(going_up, axis, [(d, (d + 1) % ways) for d in range(ways)])]
    ppermute x0 -> x14, starting transfers between devices: none -> 49.7 us  [the longest x6 34.4 us: ring_gather(): lax.ppermute(going_down, axis, [(d, (d - 1) % ways) for d in range(ways)])]
    all_gather x2, waiting for transfers between devices: 83.9 us -> 40.7 us  [gather_layer(): lax.all_gather(out_weight[layer], 'shard', axis=0, tiled=True)]
    unnamed x4, blocking collectives: 114 us -> 157 us
    all_gather x2, waiting for transfers between devices: 84.1 us -> 46.2 us  [gather_layer(): lax.all_gather(in_weight[layer], 'shard', axis=0, tiled=True)]
    unnamed x17, waiting for transfers between devices: 1.28 us -> 26.9 us
  transfers between devices with their start and end apart: 20 -> 34, of which waited for: 13 -> 18; matrix products, arithmetic and copies ran while one was open for 17% -> 21% of each run, Pallas kernels for 0% -> 0%
where the time goes in v1:
time: 1860 us; the launch traced here: 1850 us
  waiting for transfers between devices  1010 us (54%)
  blocking collectives  294 us (16%)
  local copies, waits for them, and re-layouts  235 us (13%)
  other arithmetic  117 us (6%)
  matrix products  111 us (6%)
  starting transfers between devices  63.2 us (3%)
  between operations  24.3 us (1%)
    reduce_scatter x2, waiting for transfers between devices, per_device(): lax.psum_scatter(g_in, 'shard', scatter_dimension=0, tiled=True)  366 us
    all_gather x4, waiting for transfers between devices, carried_in(): gathered = jax.tree.map(lambda a: lax.all_gather(a, axis), part)  227 us
    unnamed x4, blocking collectives  157 us
    reduce_scatter x2, waiting for transfers between devices, per_device(): lax.psum_scatter(g_out, 'shard', scatter_dimension=0, tiled=True)  152 us
    all_gather x2, blocking collectives, gather_layer(): lax.all_gather(conv_weight[layer], 'shard', axis=1, tiled=True)  84.9 us
    ppermute x8, waiting for transfers between devices, ring_gather(): lax.ppermute(going_up, axis, [(d, (d + 1) % ways) for d in range(ways)])  83.2 us
    slice x2, local copies, waits for them, and re-layouts, front(): total = total + conv_w[k] * padded[k:k + length] * keeps[k][:, None]  74.9 us
    psum x1, waiting for transfers between devices, per_device(): lax.psum((shares[0], shares[1], shares[2], shares[3], shares[4], shares[5...  67.1 us
  transfers between devices with their start and end apart: 34, of which 18 were waited for; matrix products, arithmetic and copies ran while one was open for 21% of the time, Pallas kernels for 0%

profile of v1, /device:TPU:0, one launch (start us, length us, event | category | flops | bytes accessed | tf_op | source)
XLA Modules:
  0.0 1854.9 jit_solution(3966138821309934395)
XLA Ops:
  21.6 51.6 %all-reduce.43 = (bf16[768]{0:T(1024)(128)(2,1)S(1)}, bf16[1792]{0:T(1024)(128)(2,1)S(1)}, bf16[1536]{0:T(1024)(128)(2,1)}, bf16[768]{0:T(1024)(128)(2,1)}, bf16...) all-reduce(bf16[768]{0:T(1024)(128)(2,1)S(1)} %dynamic-update-slice.7, ...), channel_id=4, replica_groups=mesh['rep'=4,'shard'=8] {'shard'}, use_global_device_ids=true, to_apply=%add.27 | all-reduce | flops 8192 | bytes 32768
  74.6 32.0 %all-gather.1 = bf16[1,4,1792]{1,0,2:T(2,128)(2,1)S(1)} all-gather(bf16[1,4,224]{1,0,2:T(2,128)(2,1)S(1)} %copy.431), channel_id=3, replica_groups=mesh['rep'=4,'shard'=8] {'shard'}, dimensions={2}, use_global_device_ids=true | all-gather | bytes 16128 | tf_op jit(solution)/shard_map/all_gather | solution.py:145
  107.6 37.1 %slice_reduce_fusion.7 = (f32[1792]{0:T(1024)S(1)}, f32[1792]{0:T(1024)S(1)}, f32[1792]{0:T(1024)S(1)}, f32[1792]{0:T(1024)S(1)}) fusion(f32[1,4,1792]{1,0,2:T(1,128)S(1)} %convert_element_type.131), kind=kLoop, calls=%fused_computation.124 | loop fusion | bytes 57344 | tf_op jit(solution)/shard_map/jvp()/slice | solution.py:89
  160.3 21.3 %collective-permute-done.2 = bf16[96,3352]{1,0:T(8,128)(2,1)S(1)} collective-permute-done((bf16[96,3352]{1,0:T(8,128)(2,1)S(1)}, bf16[96,3352]{1,0:T(8,128)(2,1)S(1)}, u32[]{:S(2)}, u32[]{:S(2)}) %collective-permute-start.2) | collective-permute-done | bytes 643616 | tf_op jit(solution)/shard_map/ppermute | solution.py:24
  184.0 16.8 collective-permute-start.5
  210.1 9.1 collective-permute-done.6
  253.3 52.9 %all-gather.8 = bf16[1,4,1792]{1,0,2:T(2,128)(2,1)S(1)} all-gather(bf16[1,4,224]{1,0,2:T(2,128)(2,1)S(1)} %copy.432), channel_id=10, replica_groups=mesh['rep'=4,'shard'=8] {'shard'}, dimensions={2}, use_global_device_ids=true | all-gather | bytes 16128 | tf_op jit(solution)/shard_map/all_gather | solution.py:145
  307.2 37.7 %slice_reduce_fusion.3 = (f32[1792]{0:T(1024)}, f32[1792]{0:T(1024)}, f32[1792]{0:T(1024)}, f32[1792]{0:T(1024)}) fusion(f32[1,4,1792]{1,0,2:T(1,128)S(1)} %convert_element_type.135), kind=kLoop, calls=%fused_computation.119 | loop fusion | bytes 57344 | tf_op jit(solution)/shard_map/jvp()/slice | solution.py:89
  354.5 20.9 %collective-permute-done.11 = bf16[96,3352]{1,0:T(8,128)(2,1)S(1)} collective-permute-done((bf16[96,3352]{1,0:T(8,128)(2,1)}, bf16[96,3352]{1,0:T(8,128)(2,1)S(1)}, u32[]{:S(2)}, u32[]{:S(2)}) %collective-permute-start.11) | collective-permute-done | bytes 643616 | tf_op jit(solution)/shard_map/ppermute | solution.py:24
  382.0 19.3 %collective-permute-done.13 = bf16[96,3352]{1,0:T(8,128)(2,1)S(1)} collective-permute-done((bf16[96,3352]{1,0:T(8,128)(2,1)S(1)}, bf16[96,3352]{1,0:T(8,128)(2,1)S(1)}, u32[]{:S(2)}, u32[]{:S(2)}) %collective-permute-start.13) | collective-permute-done | bytes 643616 | tf_op jit(solution)/shard_map/ppermute | solution.py:24
  405.5 9.5 collective-permute-done.15
  416.2 20.8 %all-reduce.28 = f32[192]{0:T(256)S(1)} all-reduce(f32[192]{0:T(256)S(1)} %multiply_dynamic-update-slice_fusion.1), channel_id=5, replica_groups=mesh['rep'=4,'shard'=8] {'shard'}, use_global_device_ids=true, to_apply=%add.28 | all-reduce | flops 192 | bytes 1536
  482.8 49.2 %all-reduce.32 = f32[192]{0:T(256)S(1)} all-reduce(f32[192]{0:T(256)S(1)} %multiply_dynamic-update-slice_fusion), channel_id=12, replica_groups=mesh['rep'=4,'shard'=8] {'shard'}, use_global_device_ids=true, to_apply=%add.32 | all-reduce | flops 192 | bytes 1536
  534.7 75.8 %all-gather.31.cloned.1.call-done = f32[192,128,64]{1,2,0:T(8,128)} async-done(((f32[24,128,64]{1,2,0:T(8,128)}), f32[192,128,64]{1,2,0:T(8,128)}) %all-gather.31.cloned.1.call-update) | async-done | bytes 6291472 | tf_op jit(solution)/shard_map/all_gather | solution.py:44
  622.6 40.6 %all-gather.33.cloned.1.call-done = bf16[1,1536,768]{2,1,0:T(8,128)(2,1)} async-done(((bf16[1,192,768]{2,1,0:T(8,128)(2,1)}), bf16[1,1536,768]{2,1,0:T(8,128)(2,1)}) %all-gather.33.cloned.1.call-update) | async-done | bytes 2359312 | tf_op jit(solution)/shard_map/all_gather | solution.py:144
  683.4 90.5 %all-gather.35.cloned.1.call-done = f32[192,128,64]{1,2,0:T(8,128)} async-done(((f32[24,128,64]{1,2,0:T(8,128)}), f32[192,128,64]{1,2,0:T(8,128)}) %all-gather.35.cloned.1.call-update) | async-done | bytes 6291472 | tf_op jit(solution)/shard_map/all_gather | solution.py:44
  775.2 50.7 %while.36 = (s32[]{:T(128)}, f32[24,128,64]{2,1,0:T(8,128)}, s32[]{:T(128)}, f32[8,24]{1,0:T(8,128)}, f32[8,24,128,64]{2,3,1,0:T(8,128)}, /*index=5*/s32[]{:T(128)}, s32[]{:T(128)}, s32[]{:T(128)}, s32[]{:T(128)}) while((s32[]{:T(128)}, f32[24,128,64]{2,1,0:T(8,128)}, s32[]{:T(128)}, f32[8,24]{1,0:T(8,128)}, f32[8,24,128,64]{2,3,1,0:T(8,128)}, ...), condition=%wide.region_15.17_spmd, body=%wide.region_14.16_spmd.sunk | while | flops 393222 | bytes 5505459 | solution.py:53
  895.8 6.7 fusion.169
  917.0 61.1 %all-gather.39.cloned.1.call-done = f32[192,128,64]{1,2,0:T(8,128)} async-done(((f32[24,128,64]{1,2,0:T(8,128)}), f32[192,128,64]{1,2,0:T(8,128)}) %all-gather.39.cloned.1.call-update) | async-done | bytes 6291472 | tf_op jit(solution)/shard_map/all_gather | solution.py:44
  979.4 50.2 %while.37 = (s32[]{:T(128)}, f32[24,128,64]{2,1,0:T(8,128)}, s32[]{:T(128)}, f32[8,24]{1,0:T(8,128)}, f32[8,24,128,64]{2,3,1,0:T(8,128)}, /*index=5*/s32[]{:T(128)}, s32[]{:T(128)}, s32[]{:T(128)}, s32[]{:T(128)}) while((s32[]{:T(128)}, f32[24,128,64]{2,1,0:T(8,128)}, s32[]{:T(128)}, f32[8,24]{1,0:T(8,128)}, f32[8,24,128,64]{2,3,1,0:T(8,128)}, ...), condition=%wide.region_30.32_spmd, body=%wide.region_29.31_spmd.sunk | while | flops 393222 | bytes 5505459 | solution.py:53
  1067.1 6.0 scatter-add.9
  1073.1 6.8 fusion.168
  1088.9 53.0 %reduce-scatter.17.cloned.1.call-done = f32[192,768]{1,0:T(8,128)} async-done(((f32[1536,768]{1,0:T(8,128)}), f32[192,768]{1,0:T(8,128)}) %reduce-scatter.17.cloned.1.call-update) | async-done | bytes 589840 | tf_op jit(solution)/shard_map/reduce_scatter | solution.py:250
  1141.9 98.8 %reduce-scatter.15.cloned.1.call-done = f32[192,768]{1,0:T(8,128)} async-done(((f32[1536,768]{1,0:T(8,128)}), f32[192,768]{1,0:T(8,128)}) %reduce-scatter.15.cloned.1.call-update) | async-done | bytes 589840 | tf_op jit(solution)/shard_map/reduce_scatter | solution.py:250
  1240.8 183.4 %reduce-scatter.13.cloned.1.call-done = f32[96,3352]{1,0:T(8,128)} async-done(((f32[768,3352]{1,0:T(8,128)}), f32[96,3352]{1,0:T(8,128)}) %reduce-scatter.13.cloned.1.call-update) | async-done | bytes 1287184 | tf_op jit(solution)/shard_map/reduce_scatter | solution.py:249
  1424.1 182.7 %reduce-scatter.11.cloned.1.call-done = f32[96,3352]{1,0:T(8,128)} async-done(((f32[768,3352]{1,0:T(8,128)}), f32[96,3352]{1,0:T(8,128)}) %reduce-scatter.11.cloned.1.call-update) | async-done | bytes 1287184 | tf_op jit(solution)/shard_map/reduce_scatter | solution.py:249
  1606.9 42.2 %psum.97 = f32[2,3,24]{2,1,0:T(4,128)S(1)} all-reduce(f32[2,3,24]{2,1,0:T(4,128)S(1)} %pad_maximum_fusion.11), channel_id=1, replica_groups=mesh['rep'=4,'shard'=8] {'rep','shard'}, use_global_device_ids=true, to_apply=%region_72.74 | all-reduce | flops 144 | bytes 1152 | tf_op jit(solution)/shard_map/psum | solution.py:265
  1649.7 46.2 %all-gather.41.cloned.1.call-done = bf16[1,768,3352]{2,1,0:T(8,128)(2,1)} async-done(((bf16[1,96,3352]{2,1,0:T(8,128)(2,1)}), bf16[1,768,3352]{2,1,0:T(8,128)(2,1)}) %all-gather.41.cloned.1.call-update) | async-done | bytes 5148688 | tf_op jit(solution)/shard_map/all_gather | solution.py:135
  1700.2 35.0 %all-reduce.40 = (f32[1792]{0:T(1024)S(1)}, f32[1792]{0:T(1024)S(1)}, f32[768]{0:T(1024)S(1)}, f32[768]{0:T(1024)S(1)}, f32[1536]{0:T(1024)S(1)}, /*index=5*/f32[1536]{0:T(1024)S(1)}) all-reduce(f32[1792]{0:T(1024)S(1)} %copy-done.114, f32[1792]{0:T(1024)S(1)} %copy-done.116, ...), channel_id=25, replica_groups=mesh['rep'=4,'shard'=8] {'shard'}, use_global_device_ids=true, to_apply=%region_62.64.clone | all-reduce | flops 8192 | bytes 65536
  1736.5 25.0 %reduce-scatter.19.cloned.1.call-done = f32[224,4]{1,0:T(8,128)} async-done(((f32[1792,4]{1,0:T(8,128)}), f32[224,4]{1,0:T(8,128)}) %reduce-scatter.19.cloned.1.call-update) | async-done | bytes 3600
  1762.4 10.8 all-reduce.41
  1775.6 67.1 %all-reduce.46.cloned.1.call-done = (f32[1,96,3352]{2,1,0:T(8,128)}, f32[1,96,3352]{2,1,0:T(8,128)}, f32[1,192,768]{2,1,0:T(8,128)}, f32[1,192,768]{2,1,0:T(8,128)}) async-done(((f32[1,96,3352]{2,1,0:T(8,128)}, f32[1,96,3352]{2,1,0:T(8,128)}, f32[1,192,768]{2,1,0:T(8,128)}, f32[1,192,768]{2,1,0:T(8,128)}), (f32[1,96,3352]{2,1,0:T(8,128)}, f32[1,96,3352]{2,1,0:T(8,128)}, f32[1,192,768]{2,1,0:T(8,128)}, ...) | async-done | bytes 3754000 | tf_op jit(solution)/shard_map/psum | solution.py:256
  (783 shorter events, 420.4 us)
Async XLA Ops:
  7.3 433.7 %all-gather.27.cloned.1.call-start = ((), (), s32[]{:S(2)}) async-start(), calls=%async_computation.10 | async-start | bytes 7077888 | tf_op jit(solution)/shard_map/all_gather | solution.py:44
  10.1 143.6 %collective-permute-start = (bf16[96,3352]{1,0:T(8,128)(2,1)S(1)}, bf16[96,3352]{1,0:T(8,128)(2,1)S(1)}, u32[]{:S(2)}, u32[]{:S(2)}) collective-permute-start(bf16[96,3352]{1,0:T(8,128)(2,1)S(1)} %get-tuple-element.950), channel_id=1, source_target_pairs={{0,1},{1,2},{2,3},{3,4},{4,5},{5,6},{6,7},{7,0},{8,9},{9,10},{10,1... | collective-permute-start | bytes 1930760 | tf_op jit(solution)/shard_map/ppermute | solution.py:24
  13.1 140.7 %collective-permute-start.1 = (bf16[96,3352]{1,0:T(8,128)(2,1)S(1)}, bf16[96,3352]{1,0:T(8,128)(2,1)S(1)}, u32[]{:S(2)}, u32[]{:S(2)}) collective-permute-start(bf16[96,3352]{1,0:T(8,128)(2,1)S(1)} %get-tuple-element.950), channel_id=1, source_target_pairs={{0,7},{1,0},{2,1},{3,2},{4,3},{5,4},{6,5},{7,6},{8,15},{9,8},{10,9... | collective-permute-start | bytes 1930760 | tf_op jit(solution)/shard_map/ppermute | solution.py:27
  16.2 134.8 %collective-permute-start.8 = (s32[3]{0:T(128)S(1)}, s32[3]{0:T(128)S(1)}, u32[]{:S(2)}, u32[]{:S(2)}) collective-permute-start(s32[3]{0:T(128)S(1)} %slice_bitcast_fusion.5), channel_id=1, source_target_pairs={{0,1},{1,2},{2,3},{3,4},{4,5},{5,6},{6,7},{8,9},{9,10},{10,11},{11... | collective-permute-start | bytes 44 | tf_op jit(solution)/shard_map/ppermute | solution.py:37
  153.7 27.8 %collective-permute-start.2 = (bf16[96,3352]{1,0:T(8,128)(2,1)S(1)}, bf16[96,3352]{1,0:T(8,128)(2,1)S(1)}, u32[]{:S(2)}, u32[]{:S(2)}) collective-permute-start(bf16[96,3352]{1,0:T(8,128)(2,1)S(1)} %collective-permute-done), channel_id=1, source_target_pairs={{0,1},{1,2},{2,3},{3,4},{4,5},{5,6},{6,7},{7,0},{8,9},{9,10},{10,1... | collective-permute-start | bytes 1930760 | tf_op jit(solution)/shard_map/ppermute | solution.py:24
  153.8 30.2 %collective-permute-start.3 = (bf16[96,3352]{1,0:T(8,128)(2,1)S(1)}, bf16[96,3352]{1,0:T(8,128)(2,1)S(1)}, u32[]{:S(2)}, u32[]{:S(2)}) collective-permute-start(bf16[96,3352]{1,0:T(8,128)(2,1)S(1)} %collective-permute-done.1), channel_id=1, source_target_pairs={{0,7},{1,0},{2,1},{3,2},{4,3},{5,4},{6,5},{7,6},{8,15},{9,8},{10,9... | collective-permute-start | bytes 1930760 | tf_op jit(solution)/shard_map/ppermute | solution.py:27
  181.5 24.2 %collective-permute-start.4 = (bf16[96,3352]{1,0:T(8,128)(2,1)S(1)}, bf16[96,3352]{1,0:T(8,128)(2,1)S(1)}, u32[]{:S(2)}, u32[]{:S(2)}) collective-permute-start(bf16[96,3352]{1,0:T(8,128)(2,1)S(1)} %collective-permute-done.2), channel_id=1, source_target_pairs={{0,1},{1,2},{2,3},{3,4},{4,5},{5,6},{6,7},{7,0},{8,9},{9,10},{10,1... | collective-permute-start | bytes 1930760 | tf_op jit(solution)/shard_map/ppermute | solution.py:24
  184.0 25.2 %collective-permute-start.5 = (bf16[96,3352]{1,0:T(8,128)(2,1)S(1)}, bf16[96,3352]{1,0:T(8,128)(2,1)S(1)}, u32[]{:S(2)}, u32[]{:S(2)}) collective-permute-start(bf16[96,3352]{1,0:T(8,128)(2,1)S(1)} %collective-permute-done.3), channel_id=1, source_target_pairs={{0,7},{1,0},{2,1},{3,2},{4,3},{5,4},{6,5},{7,6},{8,15},{9,8},{10,9... | collective-permute-start | bytes 1930760 | tf_op jit(solution)/shard_map/ppermute | solution.py:27
  205.8 13.4 collective-permute-start.6
  240.2 209.7 %all-gather.29.cloned.1.call-start = ((), (), s32[]{:S(2)}) async-start(), calls=%async_computation.11 | async-start | bytes 2654208 | tf_op jit(solution)/shard_map/all_gather | solution.py:144
  240.2 106.5 %collective-permute-start.9 = (bf16[96,3352]{1,0:T(8,128)(2,1)}, bf16[96,3352]{1,0:T(8,128)(2,1)}, u32[]{:S(2)}, u32[]{:S(2)}) collective-permute-start(bf16[96,3352]{1,0:T(8,128)(2,1)} %get-tuple-element.951), channel_id=1, source_target_pairs={{0,1},{1,2},{2,3},{3,4},{4,5},{5,6},{6,7},{7,0},{8,9},{9,10},{10,1... | collective-permute-start | bytes 1930760 | tf_op jit(solution)/shard_map/ppermute | solution.py:24
  242.6 106.2 %collective-permute-start.10 = (bf16[96,3352]{1,0:T(8,128)(2,1)}, bf16[96,3352]{1,0:T(8,128)(2,1)S(1)}, u32[]{:S(2)}, u32[]{:S(2)}) collective-permute-start(bf16[96,3352]{1,0:T(8,128)(2,1)} %get-tuple-element.951), channel_id=1, source_target_pairs={{0,7},{1,0},{2,1},{3,2},{4,3},{5,4},{6,5},{7,6},{8,15},{9,8},{10,9... | collective-permute-start | bytes 1930760 | tf_op jit(solution)/shard_map/ppermute | solution.py:27
  246.3 364.2 %all-gather.31.cloned.1.call-start = ((), (), s32[]{:S(2)}) async-start(), calls=%async_computation.12 | async-start | bytes 7077888 | tf_op jit(solution)/shard_map/all_gather | solution.py:44
  346.7 28.7 %collective-permute-start.11 = (bf16[96,3352]{1,0:T(8,128)(2,1)}, bf16[96,3352]{1,0:T(8,128)(2,1)S(1)}, u32[]{:S(2)}, u32[]{:S(2)}) collective-permute-start(bf16[96,3352]{1,0:T(8,128)(2,1)} %collective-permute-done.9), channel_id=1, source_target_pairs={{0,1},{1,2},{2,3},{3,4},{4,5},{5,6},{6,7},{7,0},{8,9},{9,10},{10,1... | collective-permute-start | bytes 1930760 | tf_op jit(solution)/shard_map/ppermute | solution.py:24
  348.8 29.8 %collective-permute-start.12 = (bf16[96,3352]{1,0:T(8,128)(2,1)S(1)}, bf16[96,3352]{1,0:T(8,128)(2,1)S(1)}, u32[]{:S(2)}, u32[]{:S(2)}) collective-permute-start(bf16[96,3352]{1,0:T(8,128)(2,1)S(1)} %collective-permute-done.10), channel_id=1, source_target_pairs={{0,7},{1,0},{2,1},{3,2},{4,3},{5,4},{6,5},{7,6},{8,15},{9,8},{10,9... | collective-permute-start | bytes 1930760 | tf_op jit(solution)/shard_map/ppermute | solution.py:27
  375.4 25.9 %collective-permute-start.13 = (bf16[96,3352]{1,0:T(8,128)(2,1)S(1)}, bf16[96,3352]{1,0:T(8,128)(2,1)S(1)}, u32[]{:S(2)}, u32[]{:S(2)}) collective-permute-start(bf16[96,3352]{1,0:T(8,128)(2,1)S(1)} %collective-permute-done.11), channel_id=1, source_target_pairs={{0,1},{1,2},{2,3},{3,4},{4,5},{5,6},{6,7},{7,0},{8,9},{9,10},{10,1... | collective-permute-start | bytes 1930760 | tf_op jit(solution)/shard_map/ppermute | solution.py:24
  378.6 26.0 %collective-permute-start.14 = (bf16[96,3352]{1,0:T(8,128)(2,1)S(1)}, bf16[96,3352]{1,0:T(8,128)(2,1)S(1)}, u32[]{:S(2)}, u32[]{:S(2)}) collective-permute-start(bf16[96,3352]{1,0:T(8,128)(2,1)S(1)} %collective-permute-done.12), channel_id=1, source_target_pairs={{0,7},{1,0},{2,1},{3,2},{4,3},{5,4},{6,5},{7,6},{8,15},{9,8},{10,9... | collective-permute-start | bytes 1930760 | tf_op jit(solution)/shard_map/ppermute | solution.py:27
  401.2 13.8 collective-permute-start.15
  481.9 181.3 %all-gather.33.cloned.1.call-start = ((), (), s32[]{:S(2)}) async-start(), calls=%async_computation.13 | async-start | bytes 2654208 | tf_op jit(solution)/shard_map/all_gather | solution.py:144
  482.4 291.4 %all-gather.35.cloned.1.call-start = ((), (), s32[]{:S(2)}) async-start(), calls=%async_computation.14 | async-start | bytes 7077888 | tf_op jit(solution)/shard_map/all_gather | solution.py:44
  671.4 195.7 %all-gather.37.cloned.1.call-start = ((), (), s32[]{:S(2)}) async-start(), calls=%async_computation.15 | async-start | bytes 5971968 | tf_op jit(solution)/shard_map/all_gather | solution.py:135
  672.0 306.1 %all-gather.39.cloned.1.call-start = ((), (), s32[]{:S(2)}) async-start(), calls=%async_computation.16 | async-start | bytes 7077888 | tf_op jit(solution)/shard_map/all_gather | solution.py:44
  847.4 11.3 collective-permute-start.17
  879.9 206.4 %reduce-scatter.21.cloned.1.call-start = ((), (), s32[]{:S(2)}) async-start(), calls=%async_computation.19 | async-start | bytes 1032192
  885.5 256.4 %reduce-scatter.17.cloned.1.call-start = ((), (), s32[]{:S(2)}) async-start(), calls=%async_computation.9 | async-start | bytes 5308416 | tf_op jit(solution)/shard_map/reduce_scatter | solution.py:250
  889.7 351.1 %reduce-scatter.15.cloned.1.call-start = ((), (), s32[]{:S(2)}) async-start(), calls=%async_computation.8 | async-start | bytes 5308416 | tf_op jit(solution)/shard_map/reduce_scatter | solution.py:250
  894.8 529.3 %reduce-scatter.13.cloned.1.call-start = ((), (), s32[]{:S(2)}) async-start(), calls=%async_computation.7 | async-start | bytes 11943936 | tf_op jit(solution)/shard_map/reduce_scatter | solution.py:249
  902.6 704.2 %reduce-scatter.11.cloned.1.call-start = ((), (), s32[]{:S(2)}) async-start(), calls=%async_computation.6 | async-start | bytes 11943936 | tf_op jit(solution)/shard_map/reduce_scatter | solution.py:249
  1052.3 10.6 collective-permute-start.18
  1079.9 615.9 %all-gather.41.cloned.1.call-start = ((), (), s32[]{:S(2)}) async-start(), calls=%async_computation.17 | async-start | bytes 5971968 | tf_op jit(solution)/shard_map/all_gather | solution.py:135
  1080.7 680.8 %reduce-scatter.19.cloned.1.call-start = ((), (), s32[]{:S(2)}) async-start(), calls=%async_computation.18 | async-start | bytes 1032192
  1088.8 753.9 %all-reduce.46.cloned.1.call-start = ((), (), s32[]{:S(2)}) async-start(), calls=%async_computation.20 | async-start | bytes 7667712 | tf_op jit(solution)/shard_map/psum | solution.py:256
  (212 other events, 3318.6 us)
Sparse Core Ops, SparseCore 0:
  240.3 122.7 all-gather.26
  365.9 69.4 all-gather.28
  482.0 128.5 all-gather.30
  613.2 49.9 all-gather.32
  671.5 102.2 all-gather.34
  775.9 85.5 all-gather.36
  880.0 98.0 all-gather.38
  981.4 62.0 reduce-scatter.20
  1047.2 94.6 reduce-scatter.16
  1145.4 95.2 reduce-scatter.14
  1244.4 179.7 reduce-scatter.12
  1427.6 179.1 reduce-scatter.10
  1609.0 86.8 all-gather.40
  1699.6 61.7 reduce-scatter.18
  1763.9 78.7 all-reduce.45
